TPU v7x, 256 devices: a whole 4x4x8 slice. The times are simulated.
256 devices in a mesh: row: 16 (over y_hi, x, core), col: 16 (over y_lo, z).
Axes of the slice: x: 4, y: 4 (y_hi: 2, y_lo: 2; y = y_hi * 2 + y_lo), z: 8, core: 2. Of those that a mesh axis runs over, the one named last changes fastest.
Arguments:
- pool: bfloat16 [32768, 128], P(('row', 'col')), may hold values from -6 to 6
- targets: bfloat16 [32768], P(('row', 'col')), may hold values from -15 to 15
- picks: int32 [4096], P(('row', 'col')), may hold values from 0 to 127
- inducing: float32 [8192, 128], replicated, may hold values from -6 to 6
- inv_sq_lengths: float32 [128], replicated, may hold values from 0.04 to 0.12
- prec_old: float32 [8192, 8192], P('row', 'col'), may hold values from -1 to 6, as said below
- mean_old: float32 [8192], P('row'), may hold values from -6 to 6
- panel: int32 [1], replicated, may hold values from 0 to 31
Outputs:
- prec_new: float32 [8192, 8192], P('row', 'col')
- mean_new: float32 [8192], P('row')
Inputs may be any that keep to these rules, and one draw needn't show every extreme that they name: `picks`: each entry indexes a row of the dataset block held by the same device as the entry. `prec_old`: symmetric and positive definite.
All inputs are finite; a program needn't handle non-finite values.
Results may differ from a plain program's by a relative error of at most 0.0028.
Values may be sent and summed in bfloat16 or wider, within the bound.
No kernel may reach another device: no remote copies, remote signals or barrier semaphores. Data moves between devices by JAX's collectives and lax.ppermute only.
A program may use at most 128 MiB of HBM per device.

v0:
```python
import jax
import jax.numpy as jnp
from jax import lax
from jax.sharding import Mesh
from jax.sharding import PartitionSpec as P

M = 8192
PB = 256
ROW_COL = ("row_0", "row_1", "row_2", "col_0", "col_1")
ROW = ("row_0", "row_1", "row_2")
COL = ("col_0", "col_1")
RATE = 0.5
EPSILON = 1e-05


def over_axes(value, axes):
    for axis in axes:
        value = lax.psum(value, axis)
    return value


def side_by_side(arrays, axis, dim, along):
    columns = [a.reshape(*a.shape[:along], -1) for a in arrays]
    both = jnp.concatenate(columns, axis=along)
    out, at, finished = (lax.all_gather(both, axis, axis=dim, tiled=True), 0, [])
    for a, column in zip(arrays, columns):
        slab = out[..., at : at + column.shape[along]]
        finished.append(slab.reshape(*slab.shape[:along], *a.shape[along:]))
        at += column.shape[along]
    return tuple(finished)


def in_blocks(value, dim, devices):
    shape = value.shape
    blocks = value.reshape(*shape[:dim], devices, shape[dim] // devices, *shape[dim + 1 :])
    return jnp.moveaxis(blocks, dim, 0)


def summed_on_arrival(value, axis, dim):
    blocks = in_blocks(value, dim, lax.axis_size(axis))
    arrived = lax.all_to_all(blocks, axis, split_axis=0, concat_axis=0, tiled=True)
    return arrived.sum(axis=0)


def picked(value, axis, root):
    return lax.dynamic_index_in_dim(lax.all_gather(value, axis), root, 0, keepdims=False)


def kernel_block(points, weights, sample_x):
    sample_f = sample_x.astype(jnp.float32)
    point_sq = jnp.sum(points * points * weights, axis=1)
    sample_sq = jnp.sum(sample_f * sample_f * weights, axis=1)
    cross_term = lax.dot_general(
        points * weights, sample_f, (((1,), (1,)), ((), ())), precision=lax.Precision.HIGHEST
    )
    return jnp.exp(-0.5 * (point_sq[:, None] + sample_sq[None, :] - 2.0 * cross_term)).astype(
        jnp.bfloat16
    )


def local_diag(gram_tile, row_base, col_base):
    row_ids = row_base + jnp.arange(gram_tile.shape[0], dtype=jnp.int32)
    col_ids = col_base + jnp.arange(gram_tile.shape[1], dtype=jnp.int32)
    on_diag = row_ids[:, None] == col_ids[None, :]
    return jnp.sum(jnp.where(on_diag, gram_tile, 0.0))


def diag_total(gram_tile, row_base, col_base):
    return over_axes(local_diag(gram_tile, row_base, col_base), ROW_COL)


def local(pool, targets, picks, inducing, inv_sq_lengths, prec_old, mean_old, panel):
    n_rows = lax.axis_size(ROW)
    n_cols = lax.axis_size(COL)
    my_row = lax.axis_index(ROW)
    my_col = lax.axis_index(COL)
    tile_rows, tile_cols = prec_old.shape
    batch_count = picks.shape[0] * n_rows * n_cols
    row_base = my_row * tile_rows
    col_base = my_col * tile_cols
    samples = jnp.take(pool, picks, axis=0)
    values = jnp.take(targets, picks, axis=0)
    group_x, group_y = side_by_side((samples, values), COL, 0, 1)
    features = kernel_block(inducing, inv_sq_lengths, group_x)
    feat_cols = lax.dynamic_slice_in_dim(features, col_base, tile_cols, 0)
    own_y = values.astype(jnp.float32)
    power_sum = over_axes(jnp.sum(own_y * own_y), ROW_COL)
    gram_tile = lax.psum_scatter(
        lax.dot_general(
            features, feat_cols, (((1,), (1,)), ((), ())), preferred_element_type=jnp.float32
        ),
        ROW,
        scatter_dimension=0,
        tiled=True,
    )
    fit_part = summed_on_arrival(
        jnp.dot(features, group_y, preferred_element_type=jnp.float32), ROW, 0
    )
    trace_sum = diag_total(gram_tile, row_base, col_base)
    trace_scale = trace_sum / M
    joined = (1.0 - RATE) * prec_old + RATE * gram_tile / trace_scale
    mean_mid = (1.0 - RATE) * mean_old + RATE * fit_part / jnp.sqrt(
        trace_scale * (power_sum / batch_count + EPSILON)
    )
    panel_start = panel[0] * PB
    owner_row = panel_start // tile_rows
    owner_col = panel_start // tile_cols
    offset_row = panel_start - owner_row * tile_rows
    offset_col = panel_start - owner_col * tile_cols
    zero_index = jnp.zeros((), jnp.int32)
    col_piece = lax.dynamic_slice(joined, (zero_index, offset_col), (tile_rows, PB))
    got_cols = picked(col_piece, COL, owner_col)
    row_piece = lax.dynamic_slice(joined, (offset_row, zero_index), (PB, tile_cols))
    mean_piece = lax.dynamic_slice(mean_mid, (offset_row,), (PB,))
    diag_piece = lax.dynamic_slice(got_cols, (offset_row, zero_index), (PB, PB))
    got_rows, got_mean, got_block = (
        picked(row_piece, ROW, owner_row),
        picked(mean_piece, ROW, owner_row),
        picked(diag_piece, ROW, owner_row),
    )
    factor = jnp.linalg.cholesky(got_block)
    identity = jnp.eye(PB, dtype=jnp.float32)
    inv_factor = lax.linalg.triangular_solve(factor, identity, left_side=True, lower=True)
    wide_rows = lax.dot_general(
        got_cols, inv_factor, (((1,), (1,)), ((), ())), precision=lax.Precision.HIGHEST
    )
    solved_rows = jnp.dot(inv_factor, got_rows, precision=lax.Precision.HIGHEST)
    head_part = jnp.dot(inv_factor, got_mean, precision=lax.Precision.HIGHEST)
    updated = joined - jnp.dot(wide_rows, solved_rows, precision=lax.Precision.HIGHEST)
    in_col = my_col == owner_col
    in_row = my_row == owner_row
    updated = jnp.where(
        in_col, lax.dynamic_update_slice(updated, wide_rows, (zero_index, offset_col)), updated
    )
    updated = jnp.where(
        in_row, lax.dynamic_update_slice(updated, solved_rows, (offset_row, zero_index)), updated
    )
    updated = jnp.where(
        jnp.logical_and(in_row, in_col),
        lax.dynamic_update_slice(updated, factor, (offset_row, offset_col)),
        updated,
    )
    mean_next = mean_mid - jnp.dot(wide_rows, head_part, precision=lax.Precision.HIGHEST)
    mean_next = jnp.where(
        in_row, lax.dynamic_update_slice(mean_next, head_part, (offset_row,)), mean_next
    )
    return (updated, mean_next)


def solution(mesh):
    split = Mesh(mesh.devices.reshape(2, 4, 2, 2, 8), ("row_0", "row_1", "row_2", "col_0", "col_1"))
    return jax.shard_map(
        local,
        mesh=split,
        in_specs=(P(ROW_COL, None), P(ROW_COL), P(ROW_COL), P(), P(), P(ROW, COL), P(ROW), P()),
        out_specs=(P(ROW, COL), P(ROW)),
        check_vma=False,
    )
```

profile of v0, /device:TPU:1, one launch (start us, length us, event | category | flops | bytes accessed | tf_op | source)
XLA Modules:
  0.0 518.6 jit_solution(1494398708425106980)
XLA Ops:
  11.3 30.8 %all_gather.25 = bf16[256,129]{1,0:T(8,128)(2,1)S(1)} all-gather(bf16[16,129]{1,0:T(8,128)(2,1)S(1)} %pad_maximum_fusion.4), channel_id=1, replica_groups=mesh['row_0'=2,'row_1'=4,'row_2'=2,'col_0'=2,'col_1'=8] {'col_0','col_1'}, dimensions={0}, use_global_device_ids=true | all-gather | bytes 70176 | tf_op jit(solution)/shard_map/all_gather | solution.py:25
  42.8 3.3 multiply_reduce_fusion
  46.2 5.9 %fusion.3 = bf16[8192,256]{1,0:T(8,128)(2,1)S(1)} fusion(f32[8192,128]{1,0:T(8,128)} %param.11, f32[256]{0:T(256)S(1)} %multiply_reduce_fusion.1, f32[8192]{0:T(1024)S(1)} %multiply_reduce_fusion, f32[128]{0:T(128)S(1)} %copy-done.5, bf16[256,129]{1,0:T(8,128)(2,1)S(1)} %all_gather.25), kind=kOutput, calls=%fused_computation.8 | convolution fusion | flops 3232759808 | bytes 8488448 | tf_op jit(solution)/shard_map/dot_general | solution.py:53
  52.1 1.9 copy-done.1
  54.0 8.1 %fusion.14 = f32[8192,512]{1,0:T(8,128)} fusion(bf16[8192,256]{1,0:T(8,128)(2,1)S(1)} %fusion.3, s32[]{:T(128)S(6)} %select_n.109), kind=kOutput, calls=%fused_computation.33 | convolution fusion | flops 2147483648 | bytes 21233668 | tf_op jit(solution)/shard_map/dot_general | solution.py:89
  62.9 156.7 %reduce-scatter.2.cloned.1.call-done = f32[512,512]{1,0:T(8,128)} async-done(((f32[8192,512]{1,0:T(8,128)}), f32[512,512]{1,0:T(8,128)}) %reduce-scatter.2.cloned.1.call-update) | async-done | bytes 1048592 | tf_op jit(solution)/shard_map/reduce_scatter | solution.py:88
  219.6 2.2 select_reduce_fusion
  221.8 5.9 %all-reduce.5 = (f32[]{:T(128)}, f32[]{:T(128)}) all-reduce(f32[]{:T(128)} %select_reduce_fusion, f32[]{:T(128)} %get-tuple-element.28), channel_id=1, replica_groups=mesh['row_0'=2,'row_1'=4,'row_2'=2,'col_0'=2,'col_1'=8] {'row_0'}, use_global_device_ids=true, to_apply=%region_4.5 | all-reduce | flops 2 | bytes 16 | tf_op jit(solution)/shard_map/psum | solution.py:18
  227.6 7.2 %all-reduce.2 = (f32[]{:T(128)}, f32[]{:T(128)}) all-reduce(f32[]{:T(128)} %get-tuple-element.26, f32[]{:T(128)} %get-tuple-element.27), channel_id=1, replica_groups=mesh['row_0'=2,'row_1'=4,'row_2'=2,'col_0'=2,'col_1'=8] {'row_1'}, use_global_device_ids=true, to_apply=%region_5.6 | all-reduce | flops 2 | bytes 16 | tf_op jit(solution)/shard_map/psum | solution.py:18
  234.8 7.7 %all-reduce.4 = (f32[]{:T(128)}, f32[]{:T(128)}) all-reduce(f32[]{:T(128)} %get-tuple-element.20, f32[]{:T(128)} %get-tuple-element.21), channel_id=1, replica_groups=mesh['row_0'=2,'row_1'=4,'row_2'=2,'col_0'=2,'col_1'=8] {'row_2'}, use_global_device_ids=true, to_apply=%region_6.7 | all-reduce | flops 2 | bytes 16 | tf_op jit(solution)/shard_map/psum | solution.py:18
  242.5 4.4 all-reduce.3
  246.9 14.3 %all-reduce.1 = (f32[]{:T(128)}, f32[]{:T(128)}) all-reduce(f32[]{:T(128)} %get-tuple-element.22, f32[]{:T(128)} %get-tuple-element.23), channel_id=1, replica_groups=mesh['row_0'=2,'row_1'=4,'row_2'=2,'col_0'=2,'col_1'=8] {'col_1'}, use_global_device_ids=true, to_apply=%region_8.9 | all-reduce | flops 2 | bytes 16 | tf_op jit(solution)/shard_map/psum | solution.py:18
  264.3 100.1 %all-gather.10.cloned.1.call-done = f32[8192,256]{1,0:T(8,128)} async-done(((f32[512,256]{1,0:T(8,128)}), f32[8192,256]{1,0:T(8,128)}) %all-gather.10.cloned.1.call-update) | async-done | bytes 8388624 | tf_op jit(solution)/shard_map/all_gather | solution.py:46
  367.2 3.4 fusion.37
  371.2 7.3 %all-to-all-start = ((f32[16,1,512]{2,1,0:T(1,128)}), f32[16,1,512]{2,1,0:T(1,128)S(1)}, u32[]{:S(2)}, u32[]{:S(2)}) async-start(f32[16,1,512]{2,1,0:T(1,128)} %all_to_all.6), calls=%async_computation.1 | async-start | bytes 65536 | tf_op jit(solution)/shard_map/all_to_all | solution.py:41
  378.5 7.2 %all-to-all-done = f32[16,1,512]{2,1,0:T(1,128)S(1)} async-done(((f32[16,1,512]{2,1,0:T(1,128)}), f32[16,1,512]{2,1,0:T(1,128)S(1)}, u32[]{:S(2)}, u32[]{:S(2)}) %all-to-all-start) | async-done | bytes 32800 | tf_op jit(solution)/shard_map/all_to_all | solution.py:41
  386.6 20.6 %all-gather.3 = f32[16,1,256]{2,1,0:T(1,128)S(1)} all-gather(f32[1,1,256]{2,1,0:T(1,128)S(1)} %bitcast.74), channel_id=4, replica_groups=mesh['row_0'=2,'row_1'=4,'row_2'=2,'col_0'=2,'col_1'=8] {'row_0','row_1'..., dimensions={0}, use_global_device_ids=true | all-gather | bytes 17408 | tf_op jit(solution)/shard_map/all_gather | solution.py:46
  407.2 19.5 %all-gather.8.cloned.1.call-done = f32[16,256,256]{2,1,0:T(8,128)} async-done(((f32[1,256,256]{2,1,0:T(8,128)}), f32[16,256,256]{2,1,0:T(8,128)}) %all-gather.8.cloned.1.call-update) | async-done | bytes 4194320 | tf_op jit(solution)/shard_map/all_gather | solution.py:46
  428.9 11.7 %cholesky.50 = f32[128,128]{1,0:T(8,128)S(1)} custom-call(f32[128,128]{1,0:T(8,128)S(1)} %cholesky.118), custom_call_target="Cholesky" | custom-call | tf_op jit(solution)/shard_map/jit(cholesky)/cholesky | solution.py:121
  440.6 9.8 %custom-call.14 = f32[1,128,128]{1,2,0:T(8,128)S(1)} custom-call(f32[1,128,128]{2,1,0:T(8,128)S(1)} %get-tuple-element.35), custom_call_target="InvertDiagBlocksLowerTriangular" | custom-call | tf_op jit(solution)/shard_map/jit(cholesky)/cholesky | solution.py:121
  450.9 11.7 %cholesky.105 = f32[128,128]{1,0:T(8,128)S(1)} custom-call(f32[128,128]{1,0:T(8,128)S(1)} %convolution_subtract_fusion.2), custom_call_target="Cholesky" | custom-call | tf_op jit(solution)/shard_map/jit(cholesky)/cholesky | solution.py:121
  465.3 4.0 while.1
  469.3 19.7 %custom-call.15 = f32[2,128,128]{1,2,0:T(8,128)S(1)} custom-call(f32[2,128,128]{2,1,0:T(8,128)S(1)} %get-tuple-element.9), custom_call_target="InvertDiagBlocksLowerTriangular" | custom-call | tf_op jit(solution)/shard_map/triangular_solve | solution.py:123
  492.4 15.1 %all-gather.12.cloned.1.call-done = f32[4096,512]{1,0:T(8,128)} async-done(((f32[256,512]{1,0:T(8,128)}), f32[4096,512]{1,0:T(8,128)}) %all-gather.12.cloned.1.call-update) | async-done | bytes 8388624 | tf_op jit(solution)/shard_map/all_gather | solution.py:46
  (78 shorter events, 26.6 us)
Async XLA Ops:
  7.2 3.4 copy-start
  7.2 39.0 %copy-start.5 = (f32[128]{0:T(128)S(1)}, f32[128]{0:T(128)}, u32[]{:S(2)}) copy-start(f32[128]{0:T(128)} %param.12) | copy-start | bytes 1540
  7.2 212.4 %reduce-scatter.2.cloned.1.call-start = ((), (), s32[]{:S(2)}) async-start(), calls=%async_computation.2 | async-start | bytes 17825792 | tf_op jit(solution)/shard_map/reduce_scatter | solution.py:88
  52.1 1.9 copy-start.1
  62.1 199.8 %copy-start.3 = (f32[512,512]{1,0:T(8,128)S(1)}, f32[512,512]{1,0:T(8,128)}, u32[]{:S(2)}) copy-start(f32[512,512]{1,0:T(8,128)} %param.13) | copy-start | bytes 3145732
  62.1 302.3 %all-gather.10.cloned.1.call-start = ((), (), s32[]{:S(2)}) async-start(), calls=%async_computation.4 | async-start | bytes 8912896 | tf_op jit(solution)/shard_map/all_gather | solution.py:46
  263.4 123.1 %copy-start.6 = (f32[512]{0:T(512)S(1)}, f32[512]{0:T(512)}, u32[]{:S(2)}) copy-start(f32[512]{0:T(512)} %param.14) | copy-start | bytes 6148
  264.3 162.5 %all-gather.8.cloned.1.call-start = ((), (), s32[]{:S(2)}) async-start(), calls=%async_computation.3 | async-start | bytes 4456448 | tf_op jit(solution)/shard_map/all_gather | solution.py:46
  366.1 141.3 %all-gather.12.cloned.1.call-start = ((), (), s32[]{:S(2)}) async-start(), calls=%async_computation.5 | async-start | bytes 8912896 | tf_op jit(solution)/shard_map/all_gather | solution.py:46
  371.2 14.6 %all-to-all-start = ((f32[16,1,512]{2,1,0:T(1,128)}), f32[16,1,512]{2,1,0:T(1,128)S(1)}, u32[]{:S(2)}, u32[]{:S(2)}) async-start(f32[16,1,512]{2,1,0:T(1,128)} %all_to_all.6), calls=%async_computation.1 | async-start | bytes 65536 | tf_op jit(solution)/shard_map/all_to_all | solution.py:41
  510.5 0.6 copy-start.4
  511.1 1.0 copy-start.2
Sparse Core Ops, SparseCore 0:
  62.2 157.3 reduce-scatter.1
  264.4 100.0 all-gather.9
  367.2 59.5 all-gather.7
  429.9 77.4 all-gather.11
where the time goes:
time: 519 us
  waiting for transfers between devices  299 us (58%)
  blocking collectives  90.9 us (18%)
  other arithmetic  65.6 us (13%)
  matrix products  23.8 us (5%)
  between operations  17.4 us (3%)
  local copies, waits for them, and re-layouts  14.6 us (3%)
  starting transfers between devices  7.43 us (1%)
    reduce_scatter x1, waiting for transfers between devices, local(): lax.psum_scatter(lax.dot_general(features, feat_cols, (((1,), (1,)), ((),...  157 us
    all_gather x3, waiting for transfers between devices, picked(): lax.all_gather(value, axis)  135 us
    psum x5, blocking collectives, over_axes(): value = lax.psum(value, axis)  39.5 us
    another operation x7, other arithmetic, local(): factor = jnp.linalg.cholesky(got_block)  34.6 us
    all_gather x1, blocking collectives, side_by_side(): lax.all_gather(both, axis, axis=dim, tiled=True)  30.8 us
    all_gather x1, blocking collectives, picked(): lax.all_gather(value, axis)  20.6 us
    another operation x3, other arithmetic, local(): lax.linalg.triangular_solve(factor, identity, left_side=True, lower=True)  19.7 us
  transfers between devices with their start and end apart: 5, of which 5 were waited for; matrix products, arithmetic and copies ran while one was open for 13% of the time, Pallas kernels for 0%

commit v1 on v0

--- a/solution.py
+++ b/solution.py
@@ -15,7 +15,7 @@
 
 def over_axes(value, axes):
     for axis in axes:
-        value = lax.psum(value, axis)
+        value = jnp.sum(lax.all_gather(value, axis), axis=0)
     return value
 
 

time: 519 us -> 537 us (1.035)
  local copies, waits for them, and re-layouts: 14.6 us -> 31.5 us
  other arithmetic: 65.6 us -> 71.9 us
    psum x5 -> x0, blocking collectives: 39.5 us -> none  [over_axes(): value = lax.psum(value, axis)]
    unnamed x0 -> x5, blocking collectives: none -> 36.3 us
    unnamed x14 -> x49, local copies, waits for them, and re-layouts: 3.43 us -> 20.4 us
    reduce_sum x0 -> x10, other arithmetic: none -> 6.29 us  [over_axes(): value = jnp.sum(lax.all_gather(value, axis), axis=0)]
where the time goes in v1:
time: 537 us; the launch traced here: 536 us
  waiting for transfers between devices  296 us (55%)
  blocking collectives  87.7 us (16%)
  other arithmetic  71.9 us (13%)
  local copies, waits for them, and re-layouts  31.5 us (6%)
  matrix products  23.8 us (4%)
  between operations  17.5 us (3%)
  starting transfers between devices  7.43 us (1%)
    reduce_scatter x1, waiting for transfers between devices, local(): lax.psum_scatter(lax.dot_general(features, feat_cols, (((1,), (1,)), ((),...  155 us
    all_gather x3, waiting for transfers between devices, picked(): lax.all_gather(value, axis)  134 us
    unnamed x5, blocking collectives  36.3 us
    another operation x7, other arithmetic, local(): factor = jnp.linalg.cholesky(got_block)  34.6 us
    all_gather x1, blocking collectives, side_by_side(): lax.all_gather(both, axis, axis=dim, tiled=True)  30.8 us
    all_gather x1, blocking collectives, picked(): lax.all_gather(value, axis)  20.6 us
    unnamed x49, local copies, waits for them, and re-layouts  20.4 us
    another operation x3, other arithmetic, local(): lax.linalg.triangular_solve(factor, identity, left_side=True, lower=True)  19.7 us
  transfers between devices with their start and end apart: 5, of which 5 were waited for; matrix products, arithmetic and copies ran while one was open for 13% of the time, Pallas kernels for 0%

profile of v1, /device:TPU:1, one launch (start us, length us, event | category | flops | bytes accessed | tf_op | source)
XLA Modules:
  0.0 536.1 jit_solution(396388877098088223)
XLA Ops:
  11.3 30.8 %all_gather.85 = bf16[256,129]{1,0:T(8,128)(2,1)S(1)} all-gather(bf16[16,129]{1,0:T(8,128)(2,1)S(1)} %pad_maximum_fusion.4), channel_id=1, replica_groups=mesh['row_0'=2,'row_1'=4,'row_2'=2,'col_0'=2,'col_1'=8] {'col_0','col_1'}, dimensions={0}, use_global_device_ids=true | all-gather | bytes 70176 | tf_op jit(solution)/shard_map/all_gather | solution.py:25
  42.8 3.3 multiply_reduce_fusion
  46.2 5.9 %fusion.3 = bf16[8192,256]{1,0:T(8,128)(2,1)S(1)} fusion(f32[8192,128]{1,0:T(8,128)} %param.11, f32[256]{0:T(256)S(1)} %multiply_reduce_fusion.1, f32[8192]{0:T(1024)S(1)} %multiply_reduce_fusion, f32[128]{0:T(128)S(1)} %copy-done.5, bf16[256,129]{1,0:T(8,128)(2,1)S(1)} %all_gather.85), kind=kOutput, calls=%fused_computation.8 | convolution fusion | flops 3232759808 | bytes 8488448 | tf_op jit(solution)/shard_map/dot_general | solution.py:53
  52.1 1.9 copy-done.1
  54.0 8.1 %fusion.14 = f32[8192,512]{1,0:T(8,128)} fusion(bf16[8192,256]{1,0:T(8,128)(2,1)S(1)} %fusion.3, s32[]{:T(128)S(6)} %select_n.109), kind=kOutput, calls=%fused_computation.33 | convolution fusion | flops 2147483648 | bytes 21233668 | tf_op jit(solution)/shard_map/dot_general | solution.py:89
  65.0 154.7 %reduce-scatter.2.cloned.1.call-done = f32[512,512]{1,0:T(8,128)} async-done(((f32[8192,512]{1,0:T(8,128)}), f32[512,512]{1,0:T(8,128)}) %reduce-scatter.2.cloned.1.call-update) | async-done | bytes 1048592 | tf_op jit(solution)/shard_map/reduce_scatter | solution.py:88
  219.6 2.2 select_reduce_fusion
  223.8 5.3 all-reduce.15
  233.7 6.5 %all-reduce.12 = (f32[4]{0:T(128)S(1)}, f32[4]{0:T(128)S(1)}) all-reduce(f32[4]{0:T(128)S(1)} %dynamic-update-slice.16, f32[4]{0:T(128)S(1)} %dynamic-update-slice.21), channel_id=1, replica_groups=mesh['row_0'=2,'row_1'=4,'row_2'=2,'col_0'=2,'col_1'=8] {'row_1'}, use_global_device_ids=true, to_apply=%add.2 | all-reduce | flops 8 | bytes 64
  244.9 7.1 %all-reduce.14 = (f32[2]{0:T(128)S(1)}, f32[2]{0:T(128)S(1)}) all-reduce(f32[2]{0:T(128)S(1)} %dynamic-update-slice.17, f32[2]{0:T(128)S(1)} %dynamic-update-slice.22), channel_id=1, replica_groups=mesh['row_0'=2,'row_1'=4,'row_2'=2,'col_0'=2,'col_1'=8] {'row_2'}, use_global_device_ids=true, to_apply=%add.3 | all-reduce | flops 4 | bytes 32
  256.6 3.8 all-reduce.13
  264.5 13.7 %all-reduce.11 = (f32[8]{0:T(128)S(1)}, f32[8]{0:T(128)S(1)}) all-reduce(f32[8]{0:T(128)S(1)} %dynamic-update-slice.19, f32[8]{0:T(128)S(1)} %dynamic-update-slice.24), channel_id=1, replica_groups=mesh['row_0'=2,'row_1'=4,'row_2'=2,'col_0'=2,'col_1'=8] {'col_1'}, use_global_device_ids=true, to_apply=%add.5 | all-reduce | flops 16 | bytes 128
  281.8 100.1 %all-gather.10.cloned.1.call-done = f32[8192,256]{1,0:T(8,128)} async-done(((f32[512,256]{1,0:T(8,128)}), f32[8192,256]{1,0:T(8,128)}) %all-gather.10.cloned.1.call-update) | async-done | bytes 8388624 | tf_op jit(solution)/shard_map/all_gather | solution.py:46
  384.7 3.4 fusion.37
  388.7 7.3 %all-to-all-start = ((f32[16,1,512]{2,1,0:T(1,128)}), f32[16,1,512]{2,1,0:T(1,128)S(1)}, u32[]{:S(2)}, u32[]{:S(2)}) async-start(f32[16,1,512]{2,1,0:T(1,128)} %all_to_all.6), calls=%async_computation.1 | async-start | bytes 65536 | tf_op jit(solution)/shard_map/all_to_all | solution.py:41
  396.0 7.2 %all-to-all-done = f32[16,1,512]{2,1,0:T(1,128)S(1)} async-done(((f32[16,1,512]{2,1,0:T(1,128)}), f32[16,1,512]{2,1,0:T(1,128)S(1)}, u32[]{:S(2)}, u32[]{:S(2)}) %all-to-all-start) | async-done | bytes 32800 | tf_op jit(solution)/shard_map/all_to_all | solution.py:41
  404.7 20.6 %all-gather.3 = f32[16,1,256]{2,1,0:T(1,128)S(1)} all-gather(f32[1,1,256]{2,1,0:T(1,128)S(1)} %bitcast.89), channel_id=4, replica_groups=mesh['row_0'=2,'row_1'=4,'row_2'=2,'col_0'=2,'col_1'=8] {'row_0','row_1'..., dimensions={0}, use_global_device_ids=true | all-gather | bytes 17408 | tf_op jit(solution)/shard_map/all_gather | solution.py:46
  425.3 18.9 %all-gather.8.cloned.1.call-done = f32[16,256,256]{2,1,0:T(8,128)} async-done(((f32[1,256,256]{2,1,0:T(8,128)}), f32[16,256,256]{2,1,0:T(8,128)}) %all-gather.8.cloned.1.call-update) | async-done | bytes 4194320 | tf_op jit(solution)/shard_map/all_gather | solution.py:46
  446.4 11.7 %cholesky.50 = f32[128,128]{1,0:T(8,128)S(1)} custom-call(f32[128,128]{1,0:T(8,128)S(1)} %cholesky.118), custom_call_target="Cholesky" | custom-call | tf_op jit(solution)/shard_map/jit(cholesky)/cholesky | solution.py:121
  458.1 9.8 %custom-call.14 = f32[1,128,128]{1,2,0:T(8,128)S(1)} custom-call(f32[1,128,128]{2,1,0:T(8,128)S(1)} %get-tuple-element.35), custom_call_target="InvertDiagBlocksLowerTriangular" | custom-call | tf_op jit(solution)/shard_map/jit(cholesky)/cholesky | solution.py:121
  468.4 11.7 %cholesky.105 = f32[128,128]{1,0:T(8,128)S(1)} custom-call(f32[128,128]{1,0:T(8,128)S(1)} %convolution_subtract_fusion.2), custom_call_target="Cholesky" | custom-call | tf_op jit(solution)/shard_map/jit(cholesky)/cholesky | solution.py:121
  482.8 4.0 while.1
  486.8 19.7 %custom-call.15 = f32[2,128,128]{1,2,0:T(8,128)S(1)} custom-call(f32[2,128,128]{2,1,0:T(8,128)S(1)} %get-tuple-element.9), custom_call_target="InvertDiagBlocksLowerTriangular" | custom-call | tf_op jit(solution)/shard_map/triangular_solve | solution.py:123
  509.9 15.1 %all-gather.12.cloned.1.call-done = f32[4096,512]{1,0:T(8,128)} async-done(((f32[256,512]{1,0:T(8,128)}), f32[4096,512]{1,0:T(8,128)}) %all-gather.12.cloned.1.call-update) | async-done | bytes 8388624 | tf_op jit(solution)/shard_map/all_gather | solution.py:46
  (123 shorter events, 49.8 us)
Async XLA Ops:
  7.2 3.4 copy-start
  7.2 39.0 %copy-start.5 = (f32[128]{0:T(128)S(1)}, f32[128]{0:T(128)}, u32[]{:S(2)}) copy-start(f32[128]{0:T(128)} %param.12) | copy-start | bytes 1540
  7.2 212.5 %reduce-scatter.2.cloned.1.call-start = ((), (), s32[]{:S(2)}) async-start(), calls=%async_computation.2 | async-start | bytes 17825792 | tf_op jit(solution)/shard_map/reduce_scatter | solution.py:88
  52.1 1.9 copy-start.1
  62.1 0.9 copy-start.11
  62.1 161.1 %copy-start.10 = (u32[256]{0:T(256)S(1)}, u32[256]{0:T(256)}, u32[]{:S(2)}) copy-start(u32[256]{0:T(256)} %constant.228) | copy-start | bytes 3076
  62.1 171.0 %copy-start.9 = (u32[256]{0:T(256)S(1)}, u32[256]{0:T(256)}, u32[]{:S(2)}) copy-start(u32[256]{0:T(256)} %constant.233) | copy-start | bytes 3076
  62.1 182.2 %copy-start.8 = (u32[256]{0:T(256)S(1)}, u32[256]{0:T(256)}, u32[]{:S(2)}) copy-start(u32[256]{0:T(256)} %constant.238) | copy-start | bytes 3076
  62.1 194.0 %copy-start.7 = (u32[256]{0:T(256)S(1)}, u32[256]{0:T(256)}, u32[]{:S(2)}) copy-start(u32[256]{0:T(256)} %constant.243) | copy-start | bytes 3076
  62.1 217.3 %copy-start.3 = (f32[512,512]{1,0:T(8,128)S(1)}, f32[512,512]{1,0:T(8,128)}, u32[]{:S(2)}) copy-start(f32[512,512]{1,0:T(8,128)} %param.13) | copy-start | bytes 3145732
  62.1 319.8 %all-gather.10.cloned.1.call-start = ((), (), s32[]{:S(2)}) async-start(), calls=%async_computation.4 | async-start | bytes 8912896 | tf_op jit(solution)/shard_map/all_gather | solution.py:46
  280.9 123.7 %copy-start.6 = (f32[512]{0:T(512)S(1)}, f32[512]{0:T(512)}, u32[]{:S(2)}) copy-start(f32[512]{0:T(512)} %param.14) | copy-start | bytes 6148
  281.8 162.5 %all-gather.8.cloned.1.call-start = ((), (), s32[]{:S(2)}) async-start(), calls=%async_computation.3 | async-start | bytes 4456448 | tf_op jit(solution)/shard_map/all_gather | solution.py:46
  383.6 141.3 %all-gather.12.cloned.1.call-start = ((), (), s32[]{:S(2)}) async-start(), calls=%async_computation.5 | async-start | bytes 8912896 | tf_op jit(solution)/shard_map/all_gather | solution.py:46
  388.7 14.6 %all-to-all-start = ((f32[16,1,512]{2,1,0:T(1,128)}), f32[16,1,512]{2,1,0:T(1,128)S(1)}, u32[]{:S(2)}, u32[]{:S(2)}) async-start(f32[16,1,512]{2,1,0:T(1,128)} %all_to_all.6), calls=%async_computation.1 | async-start | bytes 65536 | tf_op jit(solution)/shard_map/all_to_all | solution.py:41
  528.0 0.6 copy-start.4
  528.6 1.0 copy-start.2
Sparse Core Ops, SparseCore 0:
  62.3 157.3 reduce-scatter.1
  281.9 100.0 all-gather.9
  384.7 59.5 all-gather.7
  447.4 77.4 all-gather.11
